TPU v7x, 32 devices: a whole 2x2x4 slice. The times are simulated.
32 devices in a mesh: expert: 8 (over y, x, core), tensor: 4 (over z).
Axes of the slice: x: 2, y: 2, z: 4, core: 2. Of those that a mesh axis runs over, the one named last changes fastest.
Arguments:
- tokens: bfloat16 [512, 4096], P(('expert', 'tensor')), may hold values from -6 to 6
- grad_out: bfloat16 [512, 4096], P(('expert', 'tensor')), may hold values from -1.5 to 1.5
- routes: int32 [512, 8], P(('expert', 'tensor')), may hold values from 0 to 15, all different within a row; in each aligned block of 16 rows (0 to 15, 16 to 31, ...) at most 12 rows name the same one
- gate_probs: bfloat16 [512, 8], P(('expert', 'tensor')), may hold values from 0.019897461 to 0.29882812
- w_gate: bfloat16 [16, 1536, 4096], P('expert', 'tensor'), may hold values from -0.09375 to 0.09375
- w_up: bfloat16 [16, 1536, 4096], P('expert', 'tensor'), may hold values from -0.09375 to 0.09375
- w_down: bfloat16 [16, 1536, 4096], P('expert', 'tensor'), may hold values from -0.15625 to 0.15625
Outputs:
- d_tokens: bfloat16 [512, 4096], P(('expert', 'tensor'))
- d_probs: bfloat16 [512, 8], P(('expert', 'tensor'))
- d_gate: bfloat16 [16, 1536, 4096], P('expert', 'tensor')
- d_up: bfloat16 [16, 1536, 4096], P('expert', 'tensor')
- d_down: bfloat16 [16, 1536, 4096], P('expert', 'tensor')
Inputs may be any that keep to these rules, and one draw needn't show every extreme that they name: `routes`: each token names 8 different experts. In each aligned block of 16 tokens (the tokens of one device) no expert is named by more than 12 tokens, a bound that some block reaches.
All inputs are finite; a program needn't handle non-finite values.
Results may differ from a plain program's by a relative error of at most 0.019.
Values may be sent and summed in bfloat16 or wider, within the bound.
A program may use at most 256 MiB of HBM per device.

v0:
```python
import jax
import jax.numpy as jnp
from jax import lax
from jax.sharding import PartitionSpec as P

AXES = ("expert", "tensor")


def per_device(tokens, grad_out, routes, gate_probs, w_gate, w_up, w_down):
    local, units, width = w_gate.shape
    first = lax.axis_index("expert") * local
    mine = first + jnp.arange(local, dtype=jnp.int32)
    owners = lax.axis_size("expert")
    ids = jnp.arange(local * owners, dtype=jnp.int32)
    hit = routes[:, :, None] == ids[None, None, :]
    table = jnp.sum(jnp.where(hit, gate_probs[:, :, None].astype(jnp.float32), 0.0), axis=1)
    table = table.astype(jnp.bfloat16)
    rows_x = lax.all_gather(tokens, AXES, axis=0, tiled=True)
    rows_g = lax.all_gather(grad_out, AXES, axis=0, tiled=True)
    probs = lax.all_gather(table, AXES, axis=0, tiled=True)
    probs = lax.dynamic_slice_in_dim(probs, first, local, axis=1).astype(jnp.float32)
    count = rows_x.shape[0]
    wg = w_gate.reshape(local * units, width)
    wu = w_up.reshape(local * units, width)
    wd = w_down.reshape(local * units, width)
    nt = (((1,), (1,)), ((), ()))
    tn = (((0,), (0,)), ((), ()))
    f32 = jnp.float32
    gate = lax.dot_general(rows_x, wg, nt, preferred_element_type=f32)
    up = lax.dot_general(rows_x, wu, nt, preferred_element_type=f32)
    back = lax.dot_general(rows_g, wd, nt, preferred_element_type=f32)
    sigma = jax.nn.sigmoid(gate)
    act = gate * sigma
    hidden = act * up
    p = jnp.broadcast_to(probs[:, :, None], (count, local, units)).reshape(count, local * units)
    d_hidden = p * back
    dgp = (d_hidden * up * sigma * (1.0 + gate * (1.0 - sigma))).astype(jnp.bfloat16)
    dup = (d_hidden * act).astype(jnp.bfloat16)
    hs = (hidden * p).astype(jnp.bfloat16)
    dprob = jnp.sum((hidden * back).reshape(count, local, units), axis=2)
    part = lax.dot_general(dgp, wg, (((1,), (0,)), ((), ())), preferred_element_type=f32)
    part = part + lax.dot_general(dup, wu, (((1,), (0,)), ((), ())), preferred_element_type=f32)
    d_tokens = lax.psum_scatter(part.astype(jnp.bfloat16), AXES, scatter_dimension=0, tiled=True)
    d_gate = lax.dot_general(dgp, rows_x, tn, preferred_element_type=f32).astype(jnp.bfloat16)
    d_up = lax.dot_general(dup, rows_x, tn, preferred_element_type=f32).astype(jnp.bfloat16)
    d_down = lax.dot_general(hs, rows_g, tn, preferred_element_type=f32).astype(jnp.bfloat16)
    wide = lax.dynamic_update_slice(jnp.zeros((count, local * owners), f32), dprob, (0, first))
    mineprob = lax.psum_scatter(wide.astype(jnp.bfloat16), AXES, scatter_dimension=0, tiled=True)
    d_probs = jnp.sum(jnp.where(hit, mineprob.astype(f32)[:, None, :], 0.0), axis=2).astype(
        jnp.bfloat16
    )
    shape = (local, units, width)
    return (d_tokens, d_probs, d_gate.reshape(shape), d_up.reshape(shape), d_down.reshape(shape))


def solution(mesh):
    tok = P(AXES, None)
    wt = P("expert", "tensor", None)
    return jax.shard_map(
        per_device,
        mesh=mesh,
        in_specs=(tok, tok, tok, tok, wt, wt, wt),
        out_specs=(tok, tok, wt, wt, wt),
        check_vma=False,
    )
```

profile of v0, /device:TPU:0, one launch (start us, length us, event | category | flops | bytes accessed | tf_op | source)
XLA Modules:
  0.0 514.9 jit_solution(6247129796937112394)
XLA Ops:
  7.2 0.7 all-gather.5.cloned.1.call-update
  7.9 0.7 all-gather.3.cloned.1.call-update
  8.6 0.0 reduce-scatter.5.cloned.1.call-start
  8.7 67.1 %all-gather.5.cloned.1.call-done = bf16[512,4096]{1,0:T(8,128)(2,1)} async-done(((bf16[16,4096]{1,0:T(8,128)(2,1)}), bf16[512,4096]{1,0:T(8,128)(2,1)}) %all-gather.5.cloned.1.call-update) | async-done | bytes 4194320 | tf_op jit(solution)/shard_map/all_gather | solution.py:18
  75.8 8.8 %fusion.3 = f32[512,768]{1,0:T(8,128)} fusion(bf16[512,4096]{1,0:T(8,128)(2,1)} %all-gather.5.cloned.1.call-done, bf16[768,4096]{1,0:T(8,128)(2,1)} %bitcast.33), kind=kOutput, calls=%fused_computation.15 | convolution fusion | flops 3221225472 | bytes 12058624 | tf_op jit(solution)/shard_map/dot_general | solution.py:30
  84.6 4.8 fusion.4
  89.5 50.0 %all-gather.3.cloned.1.call-done = bf16[512,4096]{1,0:T(8,128)(2,1)} async-done(((bf16[16,4096]{1,0:T(8,128)(2,1)}), bf16[512,4096]{1,0:T(8,128)(2,1)}) %all-gather.3.cloned.1.call-update) | async-done | bytes 4194320 | tf_op jit(solution)/shard_map/all_gather | solution.py:19
  139.5 9.5 %multiply_multiply_fusion = (f32[512,768]{1,0:T(8,128)S(1)}, f32[512,768]{1,0:T(8,128)}) fusion(f32[512,768]{1,0:T(8,128)} %fusion.3, f32[512,768]{1,0:T(8,128)} %fusion.4, bf16[512,4096]{1,0:T(8,128)(2,1)} %all-gather.3.cloned.1.call-done, bf16[768,4096]{1,0:T(8,128)(2,1)} %bitcast.32), kind=kOutput, calls=%fused_computation.10 | convolution fusion | flops 3223584768 | bytes 16777216 | tf_op jit(solution)/shard_map/dot_general | solution.py:31
  149.0 0.8 reshape.43
  149.8 0.7 reduce_sum.28
  150.6 0.4 dynamic_update_slice.3
  151.0 0.6 copy-done.5
  151.7 0.0 reduce-scatter.3.cloned.1.call-start
  151.7 0.1 copy.14
  151.8 0.1 copy.15
  151.9 132.3 %reduce-scatter.5.cloned.1.call-done = bf16[16,16]{1,0:T(8,128)(2,1)} async-done(((bf16[512,16]{1,0:T(8,128)(2,1)}), bf16[16,16]{1,0:T(8,128)(2,1)}) %reduce-scatter.5.cloned.1.call-update) | async-done | bytes 528 | tf_op jit(solution)/shard_map/reduce_scatter | solution.py:48
  284.2 0.8 convert_element_type.47
  285.0 0.2 select_reduce_fusion
  285.2 64.8 %all_gather.9 = bf16[512,16]{1,0:T(8,128)(2,1)S(1)} all-gather(bf16[16,16]{1,0:T(8,128)(2,1)S(1)} %get-tuple-element.11), channel_id=1, replica_groups=mesh['expert'=8,'tensor'=4] {'expert','tensor'}, dimensions={0}, use_global_device_ids=true | all-gather | bytes 16896 | tf_op jit(solution)/shard_map/all_gather | solution.py:20
  350.0 0.1 dynamic-slice_convert_fusion
  350.1 0.6 broadcast_in_dim.37
  350.7 0.1 copy.17
  350.9 0.9 multiply_convert_fusion.1
  351.8 0.5 slice-done.2
  352.3 0.9 slice-done.3
  353.2 3.5 fusion.5
  356.7 5.1 add_convert_fusion
  361.7 0.7 copy.16
  362.4 7.7 %convolution_convert_fusion.2 = bf16[768,4096]{1,0:T(8,128)(2,1)} fusion(bf16[512,768]{1,0:T(8,128)(2,1)S(1)} %get-tuple-element.13, bf16[512,4096]{1,0:T(8,128)(2,1)} %all-gather.5.cloned.1.call-done), kind=kOutput, calls=%fused_computation.3 | convolution fusion | flops 3224371200 | bytes 11272192 | tf_op jit(solution)/shard_map/dot_general | solution.py:44
  370.1 5.4 %convolution_convert_fusion.1 = bf16[768,4096]{1,0:T(8,128)(2,1)} fusion(bf16[512,768]{1,0:T(8,128)(2,1)S(1)} %get-tuple-element.12, bf16[512,4096]{1,0:T(8,128)(2,1)S(1)} %copy-done.9), kind=kOutput, calls=%fused_computation.2 | convolution fusion | flops 3224371200 | bytes 11272192 | tf_op jit(solution)/shard_map/dot_general | solution.py:45
  375.5 5.6 %convolution_convert_fusion = bf16[768,4096]{1,0:T(8,128)(2,1)} fusion(bf16[512,4096]{1,0:T(8,128)(2,1)S(1)} %copy-done.10, f32[512,768]{1,0:T(8,128)S(1)} %bitcast.31, f32[512,768]{1,0:T(8,128)S(1)} %copy-done.1, f32[512,768]{1,0:T(8,128)S(1)} %copy-done.3), kind=kOutput, calls=%fused_computation.1 | convolution fusion | flops 3227123712 | bytes 15204352 | tf_op jit(solution)/shard_map/dot_general | solution.py:46
  381.1 127.3 %reduce-scatter.3.cloned.1.call-done = bf16[16,4096]{1,0:T(8,128)(2,1)} async-done(((bf16[512,4096]{1,0:T(8,128)(2,1)}), bf16[16,4096]{1,0:T(8,128)(2,1)}) %reduce-scatter.3.cloned.1.call-update) | async-done | bytes 131088 | tf_op jit(solution)/shard_map/reduce_scatter | solution.py:43
  (39 shorter events, 0.2 us)
Async XLA Ops:
  7.2 68.7 %all-gather.5.cloned.1.call-start = ((), (), s32[]{:S(2)}) async-start(), calls=%async_computation.3 | async-start | bytes 4325376 | tf_op jit(solution)/shard_map/all_gather | solution.py:18
  7.2 77.4 %slice-start = ((s8[6291456]{0:T(1024)(128)(4,1)}), s8[2097152]{0:T(1024)(128)(4,1)S(1)}, s32[]{:S(2)}) async-start(s8[6291456]{0:T(1024)(128)(4,1)} %bitcast.24), calls=%async_computation.6 | async-start | bytes 4194304
  7.9 131.6 %all-gather.3.cloned.1.call-start = ((), (), s32[]{:S(2)}) async-start(), calls=%async_computation.2 | async-start | bytes 4325376 | tf_op jit(solution)/shard_map/all_gather | solution.py:19
  8.6 275.5 %reduce-scatter.5.cloned.1.call-start = ((), (), s32[]{:S(2)}) async-start(), calls=%async_computation.5 | async-start | bytes 135168 | tf_op jit(solution)/shard_map/reduce_scatter | solution.py:48
  75.8 8.8 %slice-start.1 = ((s8[6291456]{0:T(1024)(128)(4,1)}), s8[4194304]{0:T(1024)(128)(4,1)S(1)}, s32[]{:S(2)}) async-start(s8[6291456]{0:T(1024)(128)(4,1)} %bitcast.24), calls=%async_computation.7 | async-start | bytes 8388608
  75.8 8.8 %copy-start.8 = (bf16[512,4096]{1,0:T(8,128)(2,1)S(1)}, bf16[512,4096]{1,0:T(8,128)(2,1)}, u32[]{:S(2)}) copy-start(bf16[512,4096]{1,0:T(8,128)(2,1)} %all-gather.5.cloned.1.call-done) | copy-start | bytes 12582916
  149.0 2.7 copy-start.6
  149.0 2.8 copy-start.7
  151.0 0.7 copy-start.5
  151.7 356.7 %reduce-scatter.3.cloned.1.call-start = ((), (), s32[]{:S(2)}) async-start(), calls=%async_computation.4 | async-start | bytes 4325376 | tf_op jit(solution)/shard_map/reduce_scatter | solution.py:43
  284.2 66.7 %copy-start = (f32[512,768]{1,0:T(8,128)S(1)}, f32[512,768]{1,0:T(8,128)}, u32[]{:S(2)}) copy-start(f32[512,768]{1,0:T(8,128)} %fusion.3) | copy-start | bytes 4718596
  284.2 66.7 %copy-start.2 = (f32[512,768]{1,0:T(8,128)S(1)}, f32[512,768]{1,0:T(8,128)}, u32[]{:S(2)}) copy-start(f32[512,768]{1,0:T(8,128)} %fusion.4) | copy-start | bytes 4718596
  284.2 66.7 %copy-start.4 = (f32[512,768]{1,0:T(8,128)S(1)}, f32[512,768]{1,0:T(8,128)}, u32[]{:S(2)}) copy-start(f32[512,768]{1,0:T(8,128)} %get-tuple-element.15) | copy-start | bytes 4718596
  350.1 2.2 slice-start.2
  350.9 2.3 slice-start.3
  350.9 5.8 %slice-start.4 = ((s8[6291456]{0:T(1024)(128)(4,1)}), s8[4194304]{0:T(1024)(128)(4,1)S(1)}, s32[]{:S(2)}) async-start(s8[6291456]{0:T(1024)(128)(4,1)} %bitcast.34), calls=%async_computation.10 | async-start | bytes 8388608
  353.2 3.5 slice-start.5
  362.4 7.7 %copy-start.9 = (bf16[512,4096]{1,0:T(8,128)(2,1)S(1)}, bf16[512,4096]{1,0:T(8,128)(2,1)}, u32[]{:S(2)}) copy-start(bf16[512,4096]{1,0:T(8,128)(2,1)} %all-gather.5.cloned.1.call-done) | copy-start | bytes 12582916
  370.1 5.4 %copy-start.1 = (f32[512,768]{1,0:T(8,128)S(1)}, f32[512,768]{1,0:T(8,128)}, u32[]{:S(2)}) copy-start(f32[512,768]{1,0:T(8,128)} %fusion.3) | copy-start | bytes 4718596
  370.1 5.4 %copy-start.3 = (f32[512,768]{1,0:T(8,128)S(1)}, f32[512,768]{1,0:T(8,128)}, u32[]{:S(2)}) copy-start(f32[512,768]{1,0:T(8,128)} %fusion.4) | copy-start | bytes 4718596
  370.1 5.4 %copy-start.10 = (bf16[512,4096]{1,0:T(8,128)(2,1)S(1)}, bf16[512,4096]{1,0:T(8,128)(2,1)}, u32[]{:S(2)}) copy-start(bf16[512,4096]{1,0:T(8,128)(2,1)} %all-gather.3.cloned.1.call-done) | copy-start | bytes 12582916
Sparse Core Ops, SparseCore 0:
  11.0 64.7 all-gather.4
  78.8 60.6 all-gather.2
  151.8 132.3 reduce-scatter.4
  361.9 146.4 reduce-scatter.2
where the time goes:
time: 515 us
  waiting for transfers between devices  378 us (73%)
  blocking collectives  64.8 us (13%)
  matrix products  50.2 us (10%)
  between operations  14 us (3%)
    reduce_scatter x1, waiting for transfers between devices, per_device(): lax.psum_scatter(wide.astype(jnp.bfloat16), AXES, scatter_dimension=0, ti...  132 us
    reduce_scatter x1, waiting for transfers between devices, per_device(): lax.psum_scatter(part.astype(jnp.bfloat16), AXES, scatter_dimension=0, ti...  127 us
    all_gather x1, waiting for transfers between devices, per_device(): rows_x = lax.all_gather(tokens, AXES, axis=0, tiled=True)  67.1 us
    all_gather x1, blocking collectives, per_device(): probs = lax.all_gather(table, AXES, axis=0, tiled=True)  64.8 us
    all_gather x1, waiting for transfers between devices, per_device(): rows_g = lax.all_gather(grad_out, AXES, axis=0, tiled=True)  50 us
  transfers between devices with their start and end apart: 4, of which 4 were waited for; matrix products, arithmetic and copies ran while one was open for 6% of the time, Pallas kernels for 0%

commit v1 on v0

--- a/solution.py
+++ b/solution.py
@@ -15,8 +15,11 @@
     hit = routes[:, :, None] == ids[None, None, :]
     table = jnp.sum(jnp.where(hit, gate_probs[:, :, None].astype(jnp.float32), 0.0), axis=1)
     table = table.astype(jnp.bfloat16)
-    rows_x = lax.all_gather(tokens, AXES, axis=0, tiled=True)
-    rows_g = lax.all_gather(grad_out, AXES, axis=0, tiled=True)
+    rows_x, rows_g = jnp.split(
+        lax.all_gather(jnp.concatenate([tokens, grad_out], axis=1), AXES, axis=0, tiled=True),
+        [tokens.shape[1]],
+        axis=1,
+    )
     probs = lax.all_gather(table, AXES, axis=0, tiled=True)
     probs = lax.dynamic_slice_in_dim(probs, first, local, axis=1).astype(jnp.float32)
     count = rows_x.shape[0]

time: 515 us -> 477 us (0.926)
  waiting for transfers between devices: 378 us -> 340 us
    all_gather x2 -> x1, waiting for transfers between devices: 117 us -> 82.6 us  [per_device(): lax.all_gather(jnp.concatenate([tokens, grad_out], axis=1), AXES, axis=0,...]
  transfers between devices with their start and end apart: 4 -> 3, of which waited for: 4 -> 3; matrix products, arithmetic and copies ran while one was open for 6% -> 5% of each run, Pallas kernels for 0% -> 0%
where the time goes in v1:
time: 477 us
  waiting for transfers between devices  340 us (71%)
  blocking collectives  64.8 us (14%)
  matrix products  48.5 us (10%)
  between operations  14 us (3%)
  local copies, waits for them, and re-layouts  5.24 us (1%)
    reduce_scatter x1, waiting for transfers between devices, per_device(): lax.psum_scatter(wide.astype(jnp.bfloat16), AXES, scatter_dimension=0, ti...  132 us
    reduce_scatter x1, waiting for transfers between devices, per_device(): lax.psum_scatter(part.astype(jnp.bfloat16), AXES, scatter_dimension=0, ti...  125 us
    all_gather x1, waiting for transfers between devices, per_device(): lax.all_gather(jnp.concatenate([tokens, grad_out], axis=1), AXES, axis=0,...  82.6 us
    all_gather x1, blocking collectives, per_device(): probs = lax.all_gather(table, AXES, axis=0, tiled=True)  64.8 us
  transfers between devices with their start and end apart: 3, of which 3 were waited for; matrix products, arithmetic and copies ran while one was open for 5% of the time, Pallas kernels for 0%

profile of v1, /device:TPU:0, one launch (start us, length us, event | category | flops | bytes accessed | tf_op | source)
XLA Modules:
  0.0 476.5 jit_solution(12382491923173957074)
XLA Ops:
  7.2 0.0 all-gather.2.cloned.1.call-start
  7.2 1.7 pad_maximum_fusion
  8.9 0.0 reduce-scatter.5.cloned.1.call-start
  9.0 82.6 %all-gather.2.cloned.1.call-done = bf16[512,8192]{1,0:T(8,128)(2,1)} async-done(((bf16[16,8192]{1,0:T(8,128)(2,1)}), bf16[512,8192]{1,0:T(8,128)(2,1)}) %all-gather.2.cloned.1.call-update) | async-done | bytes 8388624 | tf_op jit(solution)/shard_map/all_gather | solution.py:19
  91.6 7.3 %fusion.7 = f32[512,768]{1,0:T(8,128)S(1)} fusion(bf16[768,4096]{1,0:T(8,128)(2,1)} %bitcast.29, bf16[512,8192]{1,0:T(8,128)(2,1)} %all-gather.2.cloned.1.call-done), kind=kOutput, calls=%fused_computation.11 | convolution fusion | flops 3221225472 | bytes 12058624 | tf_op jit(solution)/shard_map/dot_general | solution.py:33
  98.9 0.4 copy-done.10
  99.3 3.4 fusion.5
  102.8 8.0 %multiply_multiply_fusion = (f32[512,768]{1,0:T(8,128)S(1)}, f32[512,768]{1,0:T(8,128)}) fusion(f32[512,768]{1,0:T(8,128)S(1)} %fusion.7, f32[512,768]{1,0:T(8,128)S(1)} %fusion.5, bf16[768,4096]{1,0:T(8,128)(2,1)} %bitcast.28, bf16[512,8192]{1,0:T(8,128)(2,1)S(1)} %copy-done.10), kind=kOutput, calls=%fused_computation.19 | convolution fusion | flops 3223584768 | bytes 16777216 | tf_op jit(solution)/shard_map/dot_general | solution.py:34
  110.8 0.8 reshape.43
  111.7 0.7 reduce_sum.28
  112.4 0.4 dynamic_update_slice.3
  112.8 0.6 copy-done.7
  113.5 0.0 reduce-scatter.3.cloned.1.call-start
  113.5 0.1 copy.14
  113.6 0.1 copy.15
  113.7 132.4 %reduce-scatter.5.cloned.1.call-done = bf16[16,16]{1,0:T(8,128)(2,1)} async-done(((bf16[512,16]{1,0:T(8,128)(2,1)}), bf16[16,16]{1,0:T(8,128)(2,1)}) %reduce-scatter.5.cloned.1.call-update) | async-done | bytes 528 | tf_op jit(solution)/shard_map/reduce_scatter | solution.py:51
  246.1 0.8 convert_element_type.47
  246.9 0.2 select_reduce_fusion
  247.1 64.8 %all_gather.6 = bf16[512,16]{1,0:T(8,128)(2,1)S(1)} all-gather(bf16[16,16]{1,0:T(8,128)(2,1)S(1)} %get-tuple-element.11), channel_id=1, replica_groups=mesh['expert'=8,'tensor'=4] {'expert','tensor'}, dimensions={0}, use_global_device_ids=true | all-gather | bytes 16896 | tf_op jit(solution)/shard_map/all_gather | solution.py:23
  311.8 0.1 dynamic-slice_convert_fusion
  311.9 0.6 broadcast_in_dim.37
  312.6 0.1 copy.17
  312.7 0.9 multiply_convert_fusion.1
  313.6 0.5 slice-done.2
  314.1 0.9 slice-done.3
  315.0 3.5 fusion.12
  318.5 5.2 %add_convert_fusion = bf16[512,4096]{1,0:T(8,128)(2,1)} fusion(f32[512,4096]{1,0:T(8,128)S(1)} %fusion.12, bf16[512,768]{1,0:T(8,128)(2,1)S(1)} %get-tuple-element.12, bf16[768,4096]{1,0:T(8,128)(2,1)S(1)} %bitcast.32), kind=kOutput, calls=%fused_computation | convolution fusion | flops 3225419776 | bytes 19660800 | tf_op jit(solution)/shard_map/dot_general | solution.py:45
  323.7 0.7 copy.16
  324.3 7.7 %convolution_convert_fusion.2 = bf16[768,4096]{1,0:T(8,128)(2,1)} fusion(bf16[512,768]{1,0:T(8,128)(2,1)S(1)} %get-tuple-element.13, bf16[512,8192]{1,0:T(8,128)(2,1)} %all-gather.2.cloned.1.call-done), kind=kOutput, calls=%fused_computation.3 | convolution fusion | flops 3224371200 | bytes 11272192 | tf_op jit(solution)/shard_map/dot_general | solution.py:47
  332.0 7.7 %convolution_convert_fusion.1 = bf16[768,4096]{1,0:T(8,128)(2,1)} fusion(bf16[512,768]{1,0:T(8,128)(2,1)S(1)} %get-tuple-element.12, bf16[512,8192]{1,0:T(8,128)(2,1)} %all-gather.2.cloned.1.call-done), kind=kOutput, calls=%fused_computation.2 | convolution fusion | flops 3224371200 | bytes 11272192 | tf_op jit(solution)/shard_map/dot_general | solution.py:48
  339.8 5.7 %convolution_convert_fusion = bf16[768,4096]{1,0:T(8,128)(2,1)} fusion(bf16[512,8192]{1,0:T(8,128)(2,1)S(1)} %bitcast.27, f32[512,768]{1,0:T(8,128)S(1)} %bitcast.25, f32[512,768]{1,0:T(8,128)S(1)} %copy-done.2, f32[512,768]{1,0:T(8,128)S(1)} %copy-done.5), kind=kOutput, calls=%fused_computation.1 | convolution fusion | flops 3227123712 | bytes 15204352 | tf_op jit(solution)/shard_map/dot_general | solution.py:49
  345.5 124.5 %reduce-scatter.3.cloned.1.call-done = bf16[16,4096]{1,0:T(8,128)(2,1)} async-done(((bf16[512,4096]{1,0:T(8,128)(2,1)}), bf16[16,4096]{1,0:T(8,128)(2,1)}) %reduce-scatter.3.cloned.1.call-update) | async-done | bytes 131088 | tf_op jit(solution)/shard_map/reduce_scatter | solution.py:46
  (42 shorter events, 0.1 us)
Async XLA Ops:
  7.2 84.5 %all-gather.2.cloned.1.call-start = ((), (), s32[]{:S(2)}) async-start(), calls=%async_computation.2 | async-start | bytes 8650752 | tf_op jit(solution)/shard_map/all_gather | solution.py:19
  8.9 90.0 %slice-start = ((s8[6291456]{0:T(1024)(128)(4,1)}), s8[2097152]{0:T(1024)(128)(4,1)S(1)}, s32[]{:S(2)}) async-start(s8[6291456]{0:T(1024)(128)(4,1)} %bitcast.18), calls=%async_computation.5 | async-start | bytes 4194304
  8.9 237.1 %reduce-scatter.5.cloned.1.call-start = ((), (), s32[]{:S(2)}) async-start(), calls=%async_computation.4 | async-start | bytes 135168 | tf_op jit(solution)/shard_map/reduce_scatter | solution.py:51
  91.6 7.3 %slice-start.1 = ((s8[6291456]{0:T(1024)(128)(4,1)}), s8[4194304]{0:T(1024)(128)(4,1)S(1)}, s32[]{:S(2)}) async-start(s8[6291456]{0:T(1024)(128)(4,1)} %bitcast.18), calls=%async_computation.6 | async-start | bytes 8388608
  91.6 7.7 %copy-start.10 = (bf16[512,8192]{1,0:T(8,128)(2,1)S(1)}, bf16[512,8192]{1,0:T(8,128)(2,1)}, u32[]{:S(2)}) copy-start(bf16[512,8192]{1,0:T(8,128)(2,1)} %all-gather.2.cloned.1.call-done) | copy-start | bytes 25165828
  98.9 3.9 copy-start
  102.8 8.0 %copy-start.3 = (f32[512,768]{1,0:T(8,128)}, f32[512,768]{1,0:T(8,128)S(1)}, u32[]{:S(2)}) copy-start(f32[512,768]{1,0:T(8,128)S(1)} %fusion.5) | copy-start | bytes 4718596
  110.8 2.7 copy-start.8
  110.8 2.8 copy-start.9
  112.8 0.7 copy-start.7
  113.5 356.5 %reduce-scatter.3.cloned.1.call-start = ((), (), s32[]{:S(2)}) async-start(), calls=%async_computation.3 | async-start | bytes 4325376 | tf_op jit(solution)/shard_map/reduce_scatter | solution.py:46
  246.1 66.6 %copy-start.1 = (f32[512,768]{1,0:T(8,128)S(1)}, f32[512,768]{1,0:T(8,128)}, u32[]{:S(2)}) copy-start(f32[512,768]{1,0:T(8,128)} %copy-done) | copy-start | bytes 4718596
  246.1 66.6 %copy-start.4 = (f32[512,768]{1,0:T(8,128)S(1)}, f32[512,768]{1,0:T(8,128)}, u32[]{:S(2)}) copy-start(f32[512,768]{1,0:T(8,128)} %copy-done.3) | copy-start | bytes 4718596
  246.1 66.6 %copy-start.6 = (f32[512,768]{1,0:T(8,128)S(1)}, f32[512,768]{1,0:T(8,128)}, u32[]{:S(2)}) copy-start(f32[512,768]{1,0:T(8,128)} %get-tuple-element.15) | copy-start | bytes 4718596
  311.9 2.2 slice-start.2
  312.7 2.3 slice-start.3
  312.7 5.8 %slice-start.6 = ((s8[6291456]{0:T(1024)(128)(4,1)}), s8[4194304]{0:T(1024)(128)(4,1)S(1)}, s32[]{:S(2)}) async-start(s8[6291456]{0:T(1024)(128)(4,1)} %bitcast.30), calls=%async_computation.11 | async-start | bytes 8388608
  315.0 3.5 slice-start.7
  324.3 15.4 %slice-start.4 = ((s8[8388608]{0:T(1024)(128)(4,1)}), s8[4194304]{0:T(1024)(128)(4,1)S(1)}, s32[]{:S(2)}) async-start(s8[8388608]{0:T(1024)(128)(4,1)} %bitcast.26), calls=%async_computation.9 | async-start | bytes 8388608
  332.0 7.7 %copy-start.2 = (f32[512,768]{1,0:T(8,128)S(1)}, f32[512,768]{1,0:T(8,128)}, u32[]{:S(2)}) copy-start(f32[512,768]{1,0:T(8,128)} %copy-done) | copy-start | bytes 4718596
  332.0 7.7 %copy-start.5 = (f32[512,768]{1,0:T(8,128)S(1)}, f32[512,768]{1,0:T(8,128)}, u32[]{:S(2)}) copy-start(f32[512,768]{1,0:T(8,128)} %copy-done.3) | copy-start | bytes 4718596
  332.0 7.7 %slice-start.5 = ((s8[8388608]{0:T(1024)(128)(4,1)}), s8[4194304]{0:T(1024)(128)(4,1)S(1)}, s32[]{:S(2)}) async-start(s8[8388608]{0:T(1024)(128)(4,1)} %bitcast.26), calls=%async_computation.10 | async-start | bytes 8388608
Sparse Core Ops, SparseCore 0:
  11.5 80.0 all-gather.1
  113.6 132.4 reduce-scatter.4
  323.8 146.1 reduce-scatter.2
